TPU v7x, 32 devices: a whole 2x2x4 slice. The times are simulated.
32 devices in a mesh: seq: 8 (over z, y), tensor: 4 (over x, core).
Axes of the slice: x: 2, y: 2, z: 4, core: 2. Of those that a mesh axis runs over, the one named last changes fastest.
Arguments:
- queries: bfloat16 [2048, 4096], P('seq', 'tensor'), may hold values from -12 to 12
- keys: bfloat16 [2048, 512], P('seq', 'tensor'), may hold values from -6 to 6
- values: bfloat16 [2048, 512], P('seq', 'tensor'), may hold values from -6 to 6
- mem_queries: bfloat16 [128, 4096], P(None, 'tensor'), may hold values from -12 to 12
- mem_proj: bfloat16 [1024, 4096], P(None, 'tensor'), may hold values from -0.09375 to 0.09375
- mem_decay: float32 [8, 1024], P('seq', 'tensor'), may hold values from 0 to 1
- pattern: int32 [8, 2, 3], P('seq'), may hold values from 0 to 1, as said below
- grad_out: bfloat16 [2048, 4096], P('seq', 'tensor'), may hold values from -6 to 6
Outputs:
- attn_out: bfloat16 [2048, 4096], P('seq', 'tensor')
- grad_queries: bfloat16 [2048, 4096], P('seq', 'tensor')
- grad_keys: bfloat16 [2048, 512], P('seq', 'tensor')
- grad_values: bfloat16 [2048, 512], P('seq', 'tensor')
Inputs may be any that keep to these rules, and one draw needn't show every extreme that they name: pattern[s, b, 0] says whether tile b of segment s reads the memory, pattern[s, b, 1 + j] whether it reads key tile j of its own segment; tile j = b is always 1 and tiles j > b are always 0.
All inputs are finite; a program needn't handle non-finite values.
Results may differ from a plain program's by a relative error of at most 0.0085.
Values sent between devices are 32-bit elements; how exact they have to be, the bound alone decides.
A program may use at most 192 MiB of HBM per device.

v0:
```python
import jax
import jax.numpy as jnp
from jax import lax
from jax.sharding import PartitionSpec as P

HD = 128
MEM = 128
BLOCK = 128


epsilon = 1e-06


def prefix(x, axis, combine, identity, reverse):
    length, mine = (lax.axis_size(axis), lax.axis_index(axis))
    everything = jax.tree.map(lambda part: lax.all_gather(part, axis), x)
    start = jax.tree.map(
        lambda part, zero: jnp.broadcast_to(jnp.asarray(zero, part.dtype), part.shape), x, identity
    )

    def lap(k, before):
        at = length - 1 - k if reverse else k
        reached = at > mine if reverse else at < mine
        new = combine(before, jax.tree.map(lambda part: part[at], everything))
        return jax.tree.map(lambda a, b: jnp.where(reached, a, b), new, before)

    return lax.fori_loop(0, length, lap, start)


def softmax_rows(scores):
    row_max = jnp.max(scores, axis=-1, keepdims=True)
    raised = jnp.exp(scores - row_max)
    return raised / jnp.sum(raised, axis=-1, keepdims=True)


def tile_mask(tile_bits, seg_len):
    expanded = jnp.repeat(jnp.repeat(tile_bits, BLOCK, axis=0), BLOCK, axis=1) > 0
    row_ids = jnp.arange(seg_len, dtype=jnp.int32)[:, None]
    col_ids = jnp.arange(MEM + seg_len, dtype=jnp.int32)[None, :]
    causal = (col_ids < MEM) | (col_ids - MEM <= row_ids)
    return expanded & causal


def chain_step(first_part, second_part):
    return (first_part[0] * second_part[0], second_part[0] * first_part[1] + second_part[1])


def read_out(mem_queries, seg_keys, seg_values):
    kv_heads = seg_keys.shape[1] // HD
    group_size = mem_queries.shape[1] // HD // kv_heads
    q_grid = mem_queries.reshape(MEM, kv_heads, group_size, HD)
    k_grid = seg_keys.reshape(-1, kv_heads, HD)
    v_grid = seg_values.reshape(-1, kv_heads, HD)
    scores = jnp.einsum(
        "qgjd,kgd->gjqk", q_grid, k_grid, preferred_element_type=jnp.float32
    ) * HD ** (-0.5)
    read_probs = softmax_rows(scores)
    read_weights = read_probs.astype(jnp.bfloat16)
    summary = jnp.einsum("gjqk,kgd->qgjd", read_weights, v_grid, preferred_element_type=jnp.float32)
    return (summary.reshape(MEM, -1).astype(jnp.bfloat16), read_probs, read_weights)


def read_back(mem_queries, seg_keys, seg_values, read_probs, read_weights, d_summary):
    kv_heads = seg_keys.shape[1] // HD
    group_size = mem_queries.shape[1] // HD // kv_heads
    q_grid = mem_queries.reshape(MEM, kv_heads, group_size, HD)
    v_grid = seg_values.reshape(-1, kv_heads, HD)
    d_grid = d_summary.reshape(MEM, kv_heads, group_size, HD)
    d_probs = jnp.einsum("qgjd,kgd->gjqk", d_grid, v_grid, preferred_element_type=jnp.float32)
    d_scores = (
        read_probs
        * (d_probs - jnp.sum(read_probs * d_probs, axis=-1, keepdims=True))
        * HD ** (-0.5)
    )
    d_scores = d_scores.astype(jnp.bfloat16)
    d_keys = jnp.einsum("gjqk,qgjd->kgd", d_scores, q_grid, preferred_element_type=jnp.float32)
    d_values = jnp.einsum(
        "gjqk,qgjd->kgd", read_weights, d_grid, preferred_element_type=jnp.float32
    )
    return (d_keys.reshape(d_keys.shape[0], -1), d_values.reshape(d_values.shape[0], -1))


def normalize(memory_state):
    state_grid = memory_state.reshape(MEM, -1, HD)
    inv_rms = lax.rsqrt(jnp.mean(state_grid * state_grid, axis=-1, keepdims=True) + epsilon)
    return (state_grid * inv_rms, inv_rms)


def memory_tokens(normed):
    split_grid = normed.reshape(MEM, -1, 2, HD)
    mem_keys = split_grid[:, :, 0, :].reshape(MEM, -1).astype(jnp.bfloat16)
    mem_values = split_grid[:, :, 1, :].reshape(MEM, -1).astype(jnp.bfloat16)
    return (mem_keys, mem_values)


def normalize_back(memory_state, inv_rms, d_mem_keys, d_mem_values):
    kv_heads = d_mem_keys.shape[1] // HD
    d_grid = jnp.stack(
        [d_mem_keys.reshape(MEM, kv_heads, HD), d_mem_values.reshape(MEM, kv_heads, HD)], axis=2
    )
    d_grid = d_grid.reshape(MEM, 2 * kv_heads, HD)
    state_grid = memory_state.reshape(MEM, -1, HD)
    d_state = inv_rms * d_grid - state_grid * inv_rms**3 * jnp.mean(
        d_grid * state_grid, axis=-1, keepdims=True
    )
    return d_state.reshape(MEM, -1)


def segment_pass(seg_queries, keys_all, values_all, live_mask, seg_grad):
    row_count = seg_queries.shape[0]
    kv_heads = keys_all.shape[1] // HD
    group_size = seg_queries.shape[1] // HD // kv_heads
    q_grid = seg_queries.reshape(row_count, kv_heads, group_size, HD)
    k_grid = keys_all.reshape(-1, kv_heads, HD)
    v_grid = values_all.reshape(-1, kv_heads, HD)
    g_grid = seg_grad.reshape(row_count, kv_heads, group_size, HD)
    scores = jnp.einsum(
        "qgjd,kgd->gjqk", q_grid, k_grid, preferred_element_type=jnp.float32
    ) * HD ** (-0.5)
    scores = jnp.where(live_mask[None, None], scores, -1e30)
    attn_probs = softmax_rows(scores)
    weights = attn_probs.astype(jnp.bfloat16)
    output = jnp.einsum("gjqk,kgd->qgjd", weights, v_grid, preferred_element_type=jnp.float32)
    d_probs = jnp.einsum("qgjd,kgd->gjqk", g_grid, v_grid, preferred_element_type=jnp.float32)
    d_scores = (
        attn_probs
        * (d_probs - jnp.sum(attn_probs * d_probs, axis=-1, keepdims=True))
        * HD ** (-0.5)
    )
    d_scores = d_scores.astype(jnp.bfloat16)
    d_queries = jnp.einsum("gjqk,kgd->qgjd", d_scores, k_grid, preferred_element_type=jnp.float32)
    d_keys = jnp.einsum("gjqk,qgjd->kgd", d_scores, q_grid, preferred_element_type=jnp.float32)
    d_values = jnp.einsum("gjqk,qgjd->kgd", weights, g_grid, preferred_element_type=jnp.float32)
    return (
        output.reshape(row_count, -1).astype(jnp.bfloat16),
        d_queries.reshape(row_count, -1).astype(jnp.bfloat16),
        d_keys.reshape(d_keys.shape[0], -1),
        d_values.reshape(d_values.shape[0], -1),
    )


def local(queries, keys, values, mem_queries, mem_proj, mem_decay, pattern, grad_out):
    seg_len = queries.shape[0]
    summary, read_probs, read_weights = read_out(mem_queries, keys, values)
    partial_value = lax.dot_general(
        summary, mem_proj, (((1,), (1,)), ((), ())), preferred_element_type=jnp.float32
    )
    mem_write = lax.psum_scatter(partial_value, "tensor", scatter_dimension=1, tiled=True)
    memory_state = prefix(
        (mem_decay, mem_write),
        "seq",
        chain_step,
        (jnp.ones_like(mem_decay), jnp.zeros_like(mem_write)),
        False,
    )[1]
    normed, inv_rms = normalize(memory_state)
    mem_keys, mem_values = memory_tokens(normed)
    keys_all = jnp.concatenate([mem_keys, keys], axis=0)
    values_all = jnp.concatenate([mem_values, values], axis=0)
    live_mask = tile_mask(pattern[0], seg_len)
    block_out = segment_pass(queries, keys_all, values_all, live_mask, grad_out)
    out_blocks = block_out[0]
    grad_blocks = block_out[1]
    key_grads = block_out[2]
    value_grads = block_out[3]
    d_state = normalize_back(memory_state, inv_rms, key_grads[:MEM], value_grads[:MEM])
    d_write = prefix(
        (mem_decay, d_state),
        "seq",
        chain_step,
        (jnp.ones_like(mem_decay), jnp.zeros_like(d_state)),
        True,
    )[1]
    d_full = lax.all_gather(d_write, "tensor", axis=1, tiled=True)
    d_summary = jnp.dot(
        d_full, mem_proj.astype(jnp.float32), precision=lax.Precision.HIGHEST
    ).astype(jnp.bfloat16)
    read_keys, read_values = read_back(
        mem_queries, keys, values, read_probs, read_weights, d_summary
    )
    grad_keys = (key_grads[MEM:] + read_keys).astype(jnp.bfloat16)
    grad_values = (value_grads[MEM:] + read_values).astype(jnp.bfloat16)
    return (out_blocks, grad_blocks, grad_keys, grad_values)


def solution(mesh):
    placed = (
        P("seq", "tensor"),
        P("seq", "tensor"),
        P("seq", "tensor"),
        P(None, "tensor"),
        P(None, "tensor"),
        P("seq", "tensor"),
        P("seq", None, None),
        P("seq", "tensor"),
    )
    return jax.shard_map(
        local,
        mesh=mesh,
        in_specs=placed,
        out_specs=(P("seq", "tensor"), P("seq", "tensor"), P("seq", "tensor"), P("seq", "tensor")),
        check_vma=False,
    )
```

profile of v0, /device:TPU:1, one launch (start us, length us, event | category | flops | bytes accessed | tf_op | source)
XLA Modules:
  0.0 178.3 jit_solution(8131560836533893034)
XLA Ops:
  7.2 1.4 fusion.56
  9.1 0.8 copy-done.3
  10.2 1.6 fusion.57
  11.9 23.6 %reduce-scatter.2.cloned.1.call-done = f32[128,256]{1,0:T(8,128)} async-done(((f32[128,1024]{1,0:T(8,128)}), f32[128,256]{1,0:T(8,128)}) %reduce-scatter.2.cloned.1.call-update) | async-done | bytes 131088 | tf_op jit(solution)/shard_map/reduce_scatter | solution.py:148
  35.6 0.7 copy.82
  36.4 2.0 %copy.120 = bf16[256,1024]{0,1:T(8,128)(2,1)} copy(bf16[256,1024]{1,0:T(8,128)(2,1)} %param.12) | data formatting | bytes 1048576 | tf_op jit(solution)/shard_map/reshape.10
  38.4 2.0 %copy.121 = bf16[256,1024]{0,1:T(8,128)(2,1)} copy(bf16[256,1024]{1,0:T(8,128)(2,1)} %param.19) | data formatting | bytes 1048576 | tf_op jit(solution)/shard_map/reshape.18
  40.7 16.8 %all-gather.3 = f32[8,1,256]{2,1,0:T(1,128)S(1)} all-gather(f32[1,1,256]{2,1,0:T(1,128)S(1)} %bitcast.263), channel_id=2, replica_groups=mesh['seq'=8,'tensor'=4] {'seq'}, dimensions={0}, use_global_device_ids=true | all-gather | bytes 9216 | tf_op jit(solution)/shard_map/all_gather | solution.py:16
  57.5 18.9 %all-gather.7.cloned.1.call-done = f32[1024,256]{1,0:T(8,128)} async-done(((f32[128,256]{1,0:T(8,128)}), f32[1024,256]{1,0:T(8,128)}) %all-gather.7.cloned.1.call-update) | async-done | bytes 1048592 | tf_op jit(solution)/shard_map/all_gather | solution.py:16
  76.5 8.1 %while.30 = (s32[]{:T(128)}, f32[128,256]{1,0:T(8,128)S(1)}, s32[]{:T(128)}, f32[8,1,256]{2,1,0:T(1,128)S(1)}, f32[8,128,256]{2,1,0:T(8,128)}, /*index=5*/s32[]{:T(128)}, s32[]{:T(128)}) while((s32[]{:T(128)}, f32[128,256]{1,0:T(8,128)S(1)}, s32[]{:T(128)}, f32[8,1,256]{2,1,0:T(1,128)S(1)}, f32[8,128,256]{2,1,0:T(8,128)}, ...), condition=%wide.region_4.5_spmd.clone, body=%wide.region_3.4_spmd.clone.sunk | while | flops 131076 | bytes 396393 | solution.py:27
  76.5 1.0 fusion.76
  77.5 1.0 fusion.76
  78.5 1.0 fusion.76
  79.5 1.0 fusion.76
  80.5 1.0 fusion.76
  81.6 1.0 fusion.76
  82.6 1.0 fusion.76
  83.6 1.0 fusion.76
  84.7 0.6 multiply_multiply_fusion
  85.3 0.8 copy.80
  86.1 1.0 multiply_convert_fusion.1
  87.1 0.6 slice_bitcast_fusion.3
  87.7 1.5 copy.81
  89.2 1.7 fusion.8
  90.9 0.7 fusion.7
  91.6 1.0 fusion.19
  92.7 1.1 fusion.2
  93.9 1.1 fusion.9
  95.0 1.1 copy-done.2
  96.2 0.6 convolution_bitcast_fusion.1
  96.8 0.7 copy-done.7
  97.5 0.7 pad_maximum_fusion
  98.2 0.6 fusion.42
  98.8 1.4 copy.91
  100.1 1.0 copy.94
  101.1 1.2 broadcast_multiply_fusion
  102.4 1.4 copy.96
  103.8 1.4 copy.95
  105.2 1.0 mul.169
  106.2 1.0 mul.162
  107.3 1.0 mul.165
  108.3 0.7 fusion.41
  109.0 2.3 %copy.101 = bf16[8,128,256]{2,0,1:T(8,128)(2,1)} copy(bf16[8,128,256]{1,2,0:T(8,128)(2,1)} %copy-done.3) | data formatting | bytes 1048576 | tf_op jit(solution)/shard_map/reshape.6
  111.3 2.7 %convolution_convert_fusion = bf16[128,8,256]{2,0,1:T(8,128)(2,1)} fusion(bf16[8,256,384]{1,2,0:T(8,128)(2,1)} %copy-done.2, bf16[256,128]{1,0:T(8,128)(2,1)} %param.13, bf16[128,128]{1,0:T(8,128)(2,1)S(1)} %get-tuple-element.300), kind=kOutput, calls=%fused_computation.26 | convolution fusion | flops 201785344 | bytes 2195456 | tf_op jit(solution)/shard_map/gjqk,kgd->qgjd/dot_general | solution.py:131
  114.0 2.0 %copy.103 = bf16[256,1024]{1,0:T(8,128)(2,1)} copy(bf16[256,1024]{0,1:T(8,128)(2,1)} %bitcast.248) | data formatting | bytes 1048576
  116.1 3.8 %fusion.15 = bf16[128,8,256]{2,0,1:T(8,128)(2,1)} fusion(bf16[256,128]{0,1:T(8,128)(2,1)S(1)} %copy-done.14, bf16[128,128]{0,1:T(8,128)(2,1)S(1)} %copy-done.20, f32[8,256]{1,0:T(8,128)S(1)} %copy-done.18, f32[8,256]{1,0:T(8,128)S(1)} %get-tuple-element.306, f32[384,256,8]{1,0,2:T(8,128)} %copy-done.1, pred[256,384]{0,1:T(8,128)(4,1)S(1)} %fusion.34), kind=kOutput, calls=%fused_computation.25 | convolution fusion | flops 205717504 | bytes 3883008 | tf_op jit(solution)/shard_map/gjqk,kgd->qgjd/dot_general | solution.py:123
  119.9 2.0 %copy.102 = bf16[256,1024]{1,0:T(8,128)(2,1)} copy(bf16[256,1024]{0,1:T(8,128)(2,1)} %bitcast.254) | data formatting | bytes 1048576
  121.9 26.2 %all-gather.9.cloned.1.call-done = f32[1024,256]{1,0:T(8,128)} async-done(((f32[128,256]{1,0:T(8,128)}), f32[1024,256]{1,0:T(8,128)}) %all-gather.9.cloned.1.call-update) | async-done | bytes 1048592 | tf_op jit(solution)/shard_map/all_gather | solution.py:16
  148.2 8.2 %while.31 = (s32[]{:T(128)}, f32[128,256]{1,0:T(8,128)S(1)}, s32[]{:T(128)}, f32[8,1,256]{2,1,0:T(1,128)S(1)}, f32[8,128,256]{2,1,0:T(8,128)}, /*index=5*/s32[]{:T(128)}, s32[]{:T(128)}, s32[]{:T(128)}, s32[]{:T(128)}) while((s32[]{:T(128)}, f32[128,256]{1,0:T(8,128)S(1)}, s32[]{:T(128)}, f32[8,1,256]{2,1,0:T(1,128)S(1)}, ...), condition=%wide.region_11.12_spmd.clone, body=%wide.region_10.11_spmd.clone.sunk | while | flops 131080 | bytes 396455 | solution.py:27
  148.2 1.0 fusion.77
  149.2 1.0 fusion.77
  150.2 1.0 fusion.77
  151.3 1.0 fusion.77
  152.3 1.0 fusion.77
  153.3 1.0 fusion.77
  154.4 1.0 fusion.77
  155.4 1.0 fusion.77
  156.4 9.4 %all_gather.25 = f32[128,1024]{1,0:T(8,128)S(1)} all-gather(f32[128,256]{1,0:T(8,128)S(1)} %get-tuple-element.231), channel_id=1, replica_groups=mesh['seq'=8,'tensor'=4] {'tensor'}, dimensions={1}, use_global_device_ids=true | all-gather | bytes 655360 | tf_op jit(solution)/shard_map/all_gather | solution.py:174
  165.8 1.0 convolution_convert_fusion.1
  166.9 1.3 multiply_reduce_fusion
  168.2 0.3 fusion.26
  168.5 0.7 copy.105
  169.3 1.7 fusion.24
  171.0 0.7 copy.104
  (85 shorter events, 1.4 us)
Async XLA Ops:
  7.2 3.0 %copy-start = (bf16[1024,1024]{1,0:T(8,128)(2,1)S(1)}, bf16[1024,1024]{1,0:T(8,128)(2,1)}, u32[]{:S(2)}) copy-start(bf16[1024,1024]{1,0:T(8,128)(2,1)} %param.16) | copy-start | bytes 6291460
  7.2 2.7 %copy-start.9 = (bf16[256,128]{1,0:T(8,128)(2,1)S(1)}, bf16[256,128]{1,0:T(8,128)(2,1)}, u32[]{:S(2)}) copy-start(bf16[256,128]{1,0:T(8,128)(2,1)} %param.14) | copy-start | bytes 196612
  7.2 28.3 %reduce-scatter.2.cloned.1.call-start = ((), (), s32[]{:S(2)}) async-start(), calls=%async_computation.1 | async-start | bytes 655360 | tf_op jit(solution)/shard_map/reduce_scatter | solution.py:148
  8.7 1.5 copy-start.15
  8.8 1.3 copy-start.21
  9.0 0.8 copy-start.3
  9.9 30.6 %copy-start.25 = (s32[1,2,3]{2,1,0:T(2,128)S(1)}, s32[1,2,3]{2,1,0:T(2,128)}, u32[]{:S(2)}) copy-start(s32[1,2,3]{2,1,0:T(2,128)} %param.18) | copy-start | bytes 76
  10.2 30.6 %copy-start.24 = (f32[1,256]{1,0:T(1,128)S(1)}, f32[1,256]{1,0:T(1,128)}, u32[]{:S(2)}) copy-start(f32[1,256]{1,0:T(1,128)} %param.17) | copy-start | bytes 3076
  11.8 64.6 %all-gather.7.cloned.1.call-start = ((), (), s32[]{:S(2)}) async-start(), calls=%async_computation.2 | async-start | bytes 1179648 | tf_op jit(solution)/shard_map/all_gather | solution.py:16
  35.6 112.6 %all-gather.9.cloned.1.call-start = ((), (), s32[]{:S(2)}) async-start(), calls=%async_computation.3 | async-start | bytes 1179648 | tf_op jit(solution)/shard_map/all_gather | solution.py:16
  85.3 0.8 copy-start.23
  89.2 2.4 %copy-start.6 = (bf16[256,1024]{0,1:T(8,128)(2,1)S(1)}, bf16[256,1024]{0,1:T(8,128)(2,1)}, u32[]{:S(2)}) copy-start(bf16[256,1024]{0,1:T(8,128)(2,1)} %copy.121) | copy-start | bytes 1572868
  90.9 2.9 %copy-start.1 = (f32[384,256,8]{1,0,2:T(8,128)}, f32[384,256,8]{1,0,2:T(8,128)S(1)}, u32[]{:S(2)}) copy-start(f32[384,256,8]{1,0,2:T(8,128)S(1)} %get-tuple-element.307) | copy-start | bytes 9437188
  91.6 2.3 %copy-start.17 = (f32[8,256]{1,0:T(8,128)}, f32[8,256]{1,0:T(8,128)S(1)}, u32[]{:S(2)}) copy-start(f32[8,256]{1,0:T(8,128)S(1)} %fusion.7) | copy-start | bytes 24580
  91.6 1.1 copy-start.13
  91.6 1.1 copy-start.19
  92.7 4.1 %copy-start.11 = (f32[384,1,128]{0,2,1:T(8,128)}, f32[384,1,128]{0,2,1:T(8,128)S(1)}, u32[]{:S(2)}) copy-start(f32[384,1,128]{0,2,1:T(8,128)S(1)} %fusion.19) | copy-start | bytes 589828
  93.9 2.3 %copy-start.4 = (bf16[256,1024]{0,1:T(8,128)(2,1)S(1)}, bf16[256,1024]{0,1:T(8,128)(2,1)}, u32[]{:S(2)}) copy-start(bf16[256,1024]{0,1:T(8,128)(2,1)} %copy.120) | copy-start | bytes 1572868
  95.0 1.2 copy-start.2
  96.8 0.7 copy-start.7
  109.0 7.1 %copy-start.14 = (bf16[256,128]{0,1:T(8,128)(2,1)S(1)}, bf16[256,128]{0,1:T(8,128)(2,1)}, u32[]{:S(2)}) copy-start(bf16[256,128]{0,1:T(8,128)(2,1)} %copy.82) | copy-start | bytes 196612
  109.0 7.1 %copy-start.18 = (f32[8,256]{1,0:T(8,128)S(1)}, f32[8,256]{1,0:T(8,128)}, u32[]{:S(2)}) copy-start(f32[8,256]{1,0:T(8,128)} %copy-done.17) | copy-start | bytes 24580
  109.0 7.1 %copy-start.20 = (bf16[128,128]{0,1:T(8,128)(2,1)S(1)}, bf16[128,128]{0,1:T(8,128)(2,1)}, u32[]{:S(2)}) copy-start(bf16[128,128]{0,1:T(8,128)(2,1)} %copy.81) | copy-start | bytes 98308
  121.9 44.9 %copy-start.10 = (bf16[256,128]{1,0:T(8,128)(2,1)S(1)}, bf16[256,128]{1,0:T(8,128)(2,1)}, u32[]{:S(2)}) copy-start(bf16[256,128]{1,0:T(8,128)(2,1)} %param.14) | copy-start | bytes 196612
  121.9 44.9 %copy-start.16 = (f32[8,128]{1,0:T(8,128)S(1)}, f32[8,128]{1,0:T(8,128)}, u32[]{:S(2)}) copy-start(f32[8,128]{1,0:T(8,128)} %copy-done.15) | copy-start | bytes 12292
  121.9 44.9 %copy-start.22 = (f32[8,128]{1,0:T(8,128)S(1)}, f32[8,128]{1,0:T(8,128)}, u32[]{:S(2)}) copy-start(f32[8,128]{1,0:T(8,128)} %copy-done.21) | copy-start | bytes 12292
  166.8 1.4 copy-start.5
  166.8 1.4 copy-start.12
  166.9 2.4 %copy-start.8 = (f32[384,1,128]{0,2,1:T(8,128)S(1)}, f32[384,1,128]{0,2,1:T(8,128)}, u32[]{:S(2)}) copy-start(f32[384,1,128]{0,2,1:T(8,128)} %copy-done.7) | copy-start | bytes 589828
Sparse Core Ops, SparseCore 0:
  12.0 23.5 reduce-scatter.1
  37.7 38.7 all-gather.6
  109.1 38.9 all-gather.8
where the time goes:
time: 179 us; the launch traced here: 178 us
  waiting for transfers between devices  68.9 us (38%)
  local copies, waits for them, and re-layouts  26.8 us (15%)
  blocking collectives  26.2 us (15%)
  other arithmetic  22.9 us (13%)
  matrix products  18.7 us (10%)
  between operations  14.2 us (8%)
    all_gather x2, waiting for transfers between devices, prefix(): everything = jax.tree.map(lambda part: lax.all_gather(part, axis), x)  45.2 us
    reduce_scatter x1, waiting for transfers between devices, local(): lax.psum_scatter(partial_value, 'tensor', scatter_dimension=1, tiled=True)  23.6 us
    all_gather x1, blocking collectives, prefix(): everything = jax.tree.map(lambda part: lax.all_gather(part, axis), x)  16.8 us
    select_n x16, other arithmetic, lap(): return jax.tree.map(lambda a, b: jnp.where(reached, a, b), new, before)  15.8 us
    all_gather x1, blocking collectives, local(): d_full = lax.all_gather(d_write, 'tensor', axis=1, tiled=True)  9.36 us
    unnamed x58, local copies, waits for them, and re-layouts  9.08 us
    another operation x3, local copies, waits for them, and re-layouts  6.34 us
    dot_general x1, matrix products, segment_pass(): jnp.einsum('gjqk,kgd->qgjd', weights, v_grid, preferred_element_type=jnp....  3.82 us
  transfers between devices with their start and end apart: 3, of which 3 were waited for; matrix products, arithmetic and copies ran while one was open for 10% of the time, Pallas kernels for 0%

commit v1 on v0

v1 whole, which is shorter than its diff:
```python
import functools

import jax
import jax.numpy as jnp
from jax import lax
from jax.experimental import pallas as pl
from jax.experimental.pallas import tpu as pltpu
from jax.sharding import PartitionSpec as P

HD = 128
MEM = 128
BLOCK = 128
EPSILON = 1e-06
DEAD = -1e30
CHUNKS = 4
SCALE = HD ** (-0.5)
F32 = jnp.float32
BF16 = jnp.bfloat16

NN = (((1,), (0,)), ((), ()))
NT = (((1,), (1,)), ((), ()))
TN = (((0,), (0,)), ((), ()))


def dot(a, b, dims):
    return lax.dot_general(a, b, dims, preferred_element_type=F32)


def heads_loop(first, last, step, fn):
    if first >= last:
        return

    def lap(i, _):
        for j in range(step):
            fn(first + i * step + j)
        return 0

    lax.fori_loop(0, (last - first) // step, lap, 0)


def kernel(
    seqs, tensors,
    q_hbm, k_hbm, v_hbm, mq_hbm, mp_hbm, decay_ref, pattern_ref, do_hbm,
    o_hbm, gq_hbm, gk_ref, gv_ref,
    q_v, k_v, v_v, mq_v, mp_v, do_v, o_v, gq_v,
    rp_v, rw_v, sum_v, bias_v, mbias_v,
    p_v, dp_v, m_v, l_v, dd_v, pm_v, dsm_v, coef_v, row_v,
    core_send, core_recv, own_part, x_send, x_recv,
    dec_own, dec_peer, w_own, w_peer, e_send, e_recv,
    state_v, mk_v, mv_v, dmk_v, dmv_v, ds_own, ds_peer, b_send, b_recv,
    r_own, ag_x, ag_core, dsum_v, dk_v, dv_v,
    load_sem, store_sem,
    core_s, core_r, x_s, x_r, dec_s, dec_r, y_s, y_r, z_s, z_r,
    by_s, by_r, bz_s, bz_r, ax_s, ax_r, ac_s, ac_r,
):
    seg = k_v.shape[0]
    group = q_v.shape[1] // HD
    width = own_part.shape[2]
    rows = MEM // CHUNKS
    half_t, half_s = tensors // 2, seqs // 2
    si, ti = lax.axis_index("seq"), lax.axis_index("tensor")
    zi, yi = si // 2, si % 2
    xi, ci = ti // 2, ti % 2
    y = yi.astype(F32)
    n_y = 1.0 - y
    core_dev = {"seq": si, "tensor": xi * 2 + (1 - ci)}
    y_dev = {"seq": zi * 2 + (1 - yi), "tensor": ti}
    up_dev = {"seq": (si + 2) % seqs, "tensor": ti}
    down_dev = {"seq": (si + seqs - 2) % seqs, "tensor": ti}
    x_devs = [{"seq": si, "tensor": ((xi + 1 + n) % half_t) * 2 + ci} for n in range(half_t - 1)]
    has_down, has_up = zi > 0, zi < half_s - 1

    def remote(src, dst, send, recv, device):
        return pltpu.make_async_remote_copy(
            src_ref=src, dst_ref=dst, send_sem=send, recv_sem=recv,
            device_id=device, device_id_type=pl.DeviceIdType.MESH,
        )

    def head(h):
        return pl.ds(pl.multiple_of(h * HD, HD), HD)

    loads = [
        pltpu.make_async_copy(src, dst, load_sem.at[n])
        for n, (src, dst) in enumerate(
            ((k_hbm, k_v), (mq_hbm, mq_v), (v_hbm, v_v), (mp_hbm, mp_v), (q_hbm, q_v), (do_hbm, do_v))
        )
    ]
    for load in loads:
        load.start()
    barrier = pltpu.get_barrier_semaphore()

    def greet(device):
        pl.semaphore_signal(barrier, inc=1, device_id=device, device_id_type=pl.DeviceIdType.MESH)

    greet(core_dev)
    greet(y_dev)
    for device in x_devs:
        greet(device)

    @pl.when(has_down)
    def _():
        greet(down_dev)

    @pl.when(has_up)
    def _():
        greet(up_dev)

    dec_own[...] = jnp.broadcast_to(decay_ref[...], dec_own.shape)

    tiles = seg // BLOCK
    tile_row = lax.broadcasted_iota(jnp.int32, (BLOCK, BLOCK), 0)
    tile_col = lax.broadcasted_iota(jnp.int32, (BLOCK, BLOCK), 1)
    diagonal = jnp.where(tile_row <= tile_col, 0.0, DEAD)
    zero_tile = jnp.zeros((BLOCK, BLOCK), F32)
    for b in range(tiles):
        at_b = slice(b * BLOCK, (b + 1) * BLOCK)
        off = (1.0 - pattern_ref[0, b, 0].astype(F32)) * DEAD
        mbias_v[:, at_b] = jnp.zeros((8, BLOCK), F32) + off
        for j in range(tiles):
            at_j = slice(j * BLOCK, (j + 1) * BLOCK)
            if j > b:
                bias_v[at_j, at_b] = zero_tile + DEAD
            else:
                off = (1.0 - pattern_ref[0, b, 1 + j].astype(F32)) * DEAD
                bias_v[at_j, at_b] = (diagonal if j == b else zero_tile) + off

    for load in loads[:3]:
        load.wait()

    def read_head(h):
        scores = dot(k_v[...], mq_v[:, head(h)], NT) * SCALE
        raised = jnp.exp(scores - jnp.max(scores, axis=0, keepdims=True))
        probs = raised / jnp.sum(raised, axis=0, keepdims=True)
        rp_v[h] = probs
        weights = probs.astype(BF16)
        rw_v[h] = weights
        sum_v[:, head(h)] = dot(weights, v_v[...], TN).astype(BF16)

    heads_loop(0, group, 4, read_head)
    loads[3].wait()

    def proj_rows(block):
        return mp_v[pl.ds(pl.multiple_of(block * width, width), width), :]

    chained = jnp.minimum(zi, 1) + jnp.minimum(half_s - 1 - zi, 1)
    pl.semaphore_wait(barrier, 2 + len(x_devs) + chained)

    sent = []
    up_sent = []
    down_sent = []

    def send(*args):
        copy = remote(*args)
        copy.start()
        sent.append(copy)

    send(dec_own, dec_peer, dec_s.at[0], dec_r.at[0], y_dev)

    for n in range(half_t):
        there = (xi + 1 + n) % half_t
        core_send[n] = dot(sum_v[...], proj_rows(there * 2 + (1 - ci)), NT)
        send(core_send.at[n], core_recv.at[n], core_s.at[n], core_r.at[n], core_dev)
    for n in range(half_t):
        there = (xi + 1 + n) % half_t
        own_part[n] = dot(sum_v[...], proj_rows(there * 2 + ci), NT)
    for n in range(half_t - 1):
        remote(core_send.at[n], core_recv.at[n], core_s.at[n], core_r.at[n], core_dev).wait_recv()
        for c in range(CHUNKS):
            at = slice(c * rows, (c + 1) * rows)
            x_send[n, c] = own_part[n, at, :] + core_recv[n, at, :]
            send(x_send.at[n, c], x_recv.at[n, c], x_s.at[n, c], x_r.at[n, c], x_devs[n])

    loads[4].wait()
    loads[5].wait()

    def own_head(h):
        scores = dot(k_v[...], q_v[:, head(h)], NT) * SCALE + bias_v[...]
        top = jnp.max(scores, axis=0, keepdims=True)
        raised = jnp.exp(scores - top)
        d_probs = dot(v_v[...], do_v[:, head(h)], NT)
        p_v[h] = raised
        dp_v[h] = d_probs
        m_v[h] = top
        l_v[h] = jnp.sum(raised, axis=0, keepdims=True)
        dd_v[h] = jnp.sum(raised * d_probs, axis=0, keepdims=True)

    heads_loop(0, group // 2, 2, own_head)

    last = half_t - 1
    remote(core_send.at[last], core_recv.at[last], core_s.at[last], core_r.at[last], core_dev).wait_recv()
    for c in range(CHUNKS):
        at = slice(c * rows, (c + 1) * rows)
        total = own_part[last, at, :] + core_recv[last, at, :]
        for n in range(half_t - 1):
            remote(x_send.at[n, c], x_recv.at[n, c], x_s.at[n, c], x_r.at[n, c], x_devs[n]).wait_recv()
            total = total + x_recv[n, c]
        w_own[c] = total
        send(w_own.at[c], w_peer.at[c], y_s.at[c], y_r.at[c], y_dev)

    heads_loop(group // 2, group, 2, own_head)

    remote(dec_own, dec_peer, dec_s.at[0], dec_r.at[0], y_dev).wait_recv()
    mine = dec_own[0:1, :]
    peer = dec_peer[0:1, :]
    both = mine * peer

    @pl.when(zi == 0)
    def _():
        e_recv[...] = jnp.zeros_like(e_recv)

    for c in range(CHUNKS):
        at = slice(c * rows, (c + 1) * rows)
        remote(w_own.at[c], w_peer.at[c], y_s.at[c], y_r.at[c], y_dev).wait_recv()
        from_peer = w_peer[c]
        pair = (n_y * peer + y) * w_own[c] + (n_y + y * mine) * from_peer
        chain = remote(e_send.at[c], e_recv.at[c], z_s.at[c], z_r.at[c], up_dev)

        @pl.when(has_down)
        def _():
            chain.wait_recv()

        entering = e_recv[c]
        e_send[c] = both * entering + pair

        @pl.when(has_up)
        def _():
            chain.start()

        up_sent.append(chain)
        state = (n_y + y * peer) * entering + y * from_peer
        state_v[at, :] = state
        for part, out in ((0, mk_v), (1, mv_v)):
            grid = state[:, part * HD : (part + 1) * HD]
            inv = lax.rsqrt(jnp.mean(grid * grid, axis=-1, keepdims=True) + EPSILON)
            out[at, :] = (grid * inv).astype(BF16)

    dmk_v[...] = jnp.zeros_like(dmk_v)
    dmv_v[...] = jnp.zeros_like(dmv_v)

    def memory_head(h):
        q_h, do_h = q_v[:, head(h)], do_v[:, head(h)]
        scores = dot(mk_v[...], q_h, NT) * SCALE + mbias_v[0:1, :]
        own_top = m_v[h]
        top = jnp.maximum(own_top, jnp.max(scores, axis=0, keepdims=True))
        shrink = jnp.exp(own_top - top)
        raised = jnp.exp(scores - top)
        inv = 1.0 / (shrink * l_v[h] + jnp.sum(raised, axis=0, keepdims=True))
        probs = raised * inv
        coef = shrink * inv
        d_probs = dot(mv_v[...], do_h, NT)
        row = coef * dd_v[h] + jnp.sum(probs * d_probs, axis=0, keepdims=True)
        d_scores = (probs * (d_probs - row) * SCALE).astype(BF16)
        weights = probs.astype(BF16)
        pm_v[h] = weights
        dsm_v[h] = d_scores
        coef_v[h] = coef
        row_v[h] = row
        dmk_v[...] += dot(d_scores, q_h, NN)
        dmv_v[...] += dot(weights, do_h, NN)

    heads_loop(0, group, 4, memory_head)

    d_state = []
    for part, grad in ((0, dmk_v), (1, dmv_v)):
        grid = state_v[:, part * HD : (part + 1) * HD]
        inv = lax.rsqrt(jnp.mean(grid * grid, axis=-1, keepdims=True) + EPSILON)
        d_normed = grad[...]
        mean = jnp.mean(d_normed * grid, axis=-1, keepdims=True)
        d_state.append(inv * d_normed - grid * (inv * inv * inv * mean))
    for c in range(CHUNKS):
        at = slice(c * rows, (c + 1) * rows)
        for part in range(2):
            ds_own[c, :, part * HD : (part + 1) * HD] = d_state[part][at, :]
        send(ds_own.at[c], ds_peer.at[c], by_s.at[c], by_r.at[c], y_dev)

    dk_v[...] = jnp.zeros_like(dk_v)
    dv_v[...] = jnp.zeros_like(dv_v)

    def grad_head(h):
        q_h, do_h = q_v[:, head(h)], do_v[:, head(h)]
        probs = p_v[h] * coef_v[h]
        d_scores = (probs * (dp_v[h] - row_v[h]) * SCALE).astype(BF16)
        weights = probs.astype(BF16)
        o_v[:, head(h)] = (dot(weights, v_v[...], TN) + dot(pm_v[h], mv_v[...], TN)).astype(BF16)
        gq_v[:, head(h)] = (dot(d_scores, k_v[...], TN) + dot(dsm_v[h], mk_v[...], TN)).astype(BF16)
        dk_v[...] += dot(d_scores, q_h, NN)
        dv_v[...] += dot(weights, do_h, NN)

    heads_loop(0, group // 2, 2, grad_head)

    @pl.when(zi == half_s - 1)
    def _():
        b_recv[...] = jnp.zeros_like(b_recv)

    for c in range(CHUNKS):
        remote(ds_own.at[c], ds_peer.at[c], by_s.at[c], by_r.at[c], y_dev).wait_recv()
        from_peer = ds_peer[c]
        pair = (y * peer + n_y) * ds_own[c] + (n_y * mine + y) * from_peer
        chain = remote(b_send.at[c], b_recv.at[c], bz_s.at[c], bz_r.at[c], down_dev)

        @pl.when(has_up)
        def _():
            chain.wait_recv()

        entering = b_recv[c]
        b_send[c] = pair + both * entering

        @pl.when(has_down)
        def _():
            chain.start()

        down_sent.append(chain)
        at = slice(c * rows, (c + 1) * rows)
        r_own[at, :] = (y + n_y * peer) * entering + n_y * from_peer
        for n in range(half_t - 1):
            send(r_own.at[pl.ds(c * rows, rows)], ag_x.at[n, pl.ds(c * rows, rows)], ax_s.at[n, c], ax_r.at[n, c], x_devs[n])
        send(r_own.at[pl.ds(c * rows, rows)], ag_core.at[0, pl.ds(c * rows, rows)], ac_s.at[0, c], ac_r.at[0, c], core_dev)

    heads_loop(group // 2, group, 2, grad_head)
    stores = [
        pltpu.make_async_copy(o_v, o_hbm, store_sem.at[0]),
        pltpu.make_async_copy(gq_v, gq_hbm, store_sem.at[1]),
    ]
    for store in stores:
        store.start()

    def back(part, block):
        high = part.astype(BF16)
        low = (part - high.astype(F32)).astype(BF16)
        proj = proj_rows(block)
        return dot(high, proj, NN) + dot(low, proj, NN)

    total = back(r_own[...], ti)
    for n in range(half_t - 1):
        for c in range(CHUNKS):
            at = pl.ds(c * rows, rows)
            remote(r_own.at[at], ag_x.at[n, at], ax_s.at[n, c], ax_r.at[n, c], x_devs[n]).wait_recv()
            send(ag_x.at[n, at], ag_core.at[1 + n, at], ac_s.at[1 + n, c], ac_r.at[1 + n, c], core_dev)
    for n in range(half_t):
        for c in range(CHUNKS):
            at = pl.ds(c * rows, rows)
            remote(r_own.at[at], ag_core.at[n, at], ac_s.at[n, c], ac_r.at[n, c], core_dev).wait_recv()
        block = (xi + half_t - n) % half_t
        total = total + back(ag_core[n], block * 2 + (1 - ci))
        if n > 0:
            total = total + back(ag_x[n - 1], block * 2 + ci)
    dsum_v[...] = total.astype(BF16)

    def back_head(h):
        d_sum = dsum_v[:, head(h)]
        probs = rp_v[h]
        d_probs = dot(v_v[...], d_sum, NT)
        d_scores = probs * (d_probs - jnp.sum(probs * d_probs, axis=0, keepdims=True)) * SCALE
        dk_v[...] += dot(d_scores.astype(BF16), mq_v[:, head(h)], NN)
        dv_v[...] += dot(rw_v[h], d_sum, NN)

    heads_loop(0, group, 4, back_head)
    gk_ref[...] = dk_v[...].astype(BF16)
    gv_ref[...] = dv_v[...].astype(BF16)

    for copy in sent:
        copy.wait_send()
    for copy in up_sent:
        @pl.when(has_up)
        def _():
            copy.wait_send()
    for copy in down_sent:
        @pl.when(has_down)
        def _():
            copy.wait_send()
    for store in stores:
        store.wait()


def local(seqs, tensors, queries, keys, values, mem_queries, mem_proj, mem_decay, pattern, grad_out):
    seg, cols = queries.shape
    width = mem_decay.shape[1]
    group = cols // HD
    half_t = tensors // 2
    rows = MEM // CHUNKS
    assert keys.shape[1] == HD and width == 2 * HD
    assert seqs % 2 == 0 and tensors % 2 == 0
    vmem = pl.BlockSpec(memory_space=pltpu.VMEM)
    anywhere = pl.BlockSpec(memory_space=pl.ANY)
    like = lambda a: pltpu.VMEM(a.shape, a.dtype)
    f32 = lambda *shape: pltpu.VMEM(shape, F32)
    b16 = lambda *shape: pltpu.VMEM(shape, BF16)
    dma = lambda *shape: pltpu.SemaphoreType.DMA(shape)
    chunk = f32(CHUNKS, rows, width)
    return pl.pallas_call(
        functools.partial(kernel, seqs, tensors),
        out_shape=tuple(jax.ShapeDtypeStruct(a.shape, BF16) for a in (grad_out, queries, keys, values)),
        in_specs=[
            anywhere, anywhere, anywhere, anywhere, anywhere, vmem,
            pl.BlockSpec(memory_space=pltpu.SMEM), anywhere,
        ],
        out_specs=(anywhere, anywhere, vmem, vmem),
        scratch_shapes=[
            like(queries), like(keys), like(values), like(mem_queries), like(mem_proj),
            like(grad_out), like(grad_out), like(queries),
            f32(group, seg, MEM), b16(group, seg, MEM), like(mem_queries), f32(seg, seg), f32(8, seg),
            f32(group, seg, seg), f32(group, seg, seg),
            f32(group, 1, seg), f32(group, 1, seg), f32(group, 1, seg),
            b16(group, MEM, seg), b16(group, MEM, seg), f32(group, 1, seg), f32(group, 1, seg),
            f32(half_t, MEM, width), f32(half_t, MEM, width), f32(half_t, MEM, width),
            f32(max(half_t - 1, 1), CHUNKS, rows, width), f32(max(half_t - 1, 1), CHUNKS, rows, width),
            f32(8, width), f32(8, width), chunk, chunk, chunk, chunk,
            f32(MEM, width), b16(MEM, HD), b16(MEM, HD), f32(MEM, HD), f32(MEM, HD),
            chunk, chunk, chunk, chunk,
            f32(MEM, width), f32(max(half_t - 1, 1), MEM, width), f32(half_t, MEM, width),
            like(mem_queries), f32(seg, HD), f32(seg, HD),
            dma(6), dma(2),
            dma(half_t), dma(half_t),
            dma(max(half_t - 1, 1), CHUNKS), dma(max(half_t - 1, 1), CHUNKS),
            dma(1), dma(1), dma(CHUNKS), dma(CHUNKS), dma(CHUNKS), dma(CHUNKS),
            dma(CHUNKS), dma(CHUNKS), dma(CHUNKS), dma(CHUNKS),
            dma(max(half_t - 1, 1), CHUNKS), dma(max(half_t - 1, 1), CHUNKS),
            dma(half_t, CHUNKS), dma(half_t, CHUNKS),
        ],
        compiler_params=pltpu.CompilerParams(collective_id=0, has_side_effects=True),
    )(queries, keys, values, mem_queries, mem_proj, mem_decay, pattern, grad_out)


def solution(mesh):
    cut = P("seq", "tensor")
    placed = (cut, cut, cut, P(None, "tensor"), P(None, "tensor"), cut, P("seq", None, None), cut)
    return jax.shard_map(
        functools.partial(local, mesh.shape["seq"], mesh.shape["tensor"]),
        mesh=mesh,
        in_specs=placed,
        out_specs=(cut, cut, cut, cut),
        check_vma=False,
    )
```

time: 179 us -> 51.4 us (0.29)
  waiting for transfers between devices: 68.9 us -> 0 us
  Pallas kernels: 0 us -> 45.5 us
  blocking collectives: 26.2 us -> 0 us
  other arithmetic: 22.9 us -> 0 us
  local copies, waits for them, and re-layouts: 26.8 us -> 5.04 us
  matrix products: 18.7 us -> 0 us
  between operations: 14.2 us -> 0.66 us
    pallas_call x0 -> x1, Pallas kernels: none -> 45.5 us  [local(): pl.pallas_call(functools.partial(kernel, seqs, tensors), out_shape=tuple(...]
    all_gather x2 -> x0, waiting for transfers between devices: 45.2 us -> none  [prefix(): everything = jax.tree.map(lambda part: lax.all_gather(part, axis), x)]
    all_gather x2 -> x0, blocking collectives: 26.2 us -> none  [the longest x1 16.8 us: prefix(): everything = jax.tree.map(lambda part: lax.all_gather(part, axis), x)]
    reduce_scatter x1 -> x0, waiting for transfers between devices: 23.6 us -> none  [local(): lax.psum_scatter(partial_value, 'tensor', scatter_dimension=1, tiled=True)]
    dot_general x13 -> x0, matrix products: 18.7 us -> none  [the longest x1 3.82 us: segment_pass(): jnp.einsum('gjqk,kgd->qgjd', weights, v_grid, preferred_element_type=jnp....]
    select_n x16 -> x0, other arithmetic: 15.8 us -> none  [lap(): return jax.tree.map(lambda a, b: jnp.where(reached, a, b), new, before)]
    another operation x4 -> x0, local copies, waits for them, and re-layouts: 6.35 us -> none
    unnamed x58 -> x8, local copies, waits for them, and re-layouts: 9.08 us -> 5.04 us
  transfers between devices with their start and end apart: 3 -> 0, of which waited for: 3 -> 0; matrix products, arithmetic and copies ran while one was open for 10% -> 0% of each run, Pallas kernels for 0% -> 0%
where the time goes in v1:
time: 51.4 us; the launch traced here: 51.2 us
  Pallas kernels  45.5 us (89%)
  local copies, waits for them, and re-layouts  5.04 us (10%)
  between operations  0.66 us (1%)
    pallas_call x1, Pallas kernels, local(): pl.pallas_call(functools.partial(kernel, seqs, tensors), out_shape=tuple(...  45.5 us
    unnamed x8, local copies, waits for them, and re-layouts  5.04 us

profile of v1, /device:TPU:1, one launch (start us, length us, event | category | flops | bytes accessed | tf_op | source)
XLA Modules:
  0.0 51.2 jit_solution(2120002150778254993)
XLA Ops:
  0.6 45.5 %shard_map.111 = (bf16[256,1024]{1,0:T(8,128)(2,1)}, bf16[256,1024]{1,0:T(8,128)(2,1)}, bf16[256,128]{1,0:T(8,128)(2,1)}, bf16[256,128]{1,0:T(8,128)(2,1)}) custom-call(bf16[256,1024]{1,0:T(8,128)(2,1)} %q_hbm.1, bf16[256,128]{1,0:T(8,128)(2,1)} %k_hbm.1, bf16[256,128]{1,0:T(8,128)(2,1)} %v_hbm.1, bf16[128,1024]{1,0:T(8,128)(2,1)} %mq_hbm.1, ...), custom_call_target="tpu_custom_call" | custom-call | tf_op jit(solution)/shard_map/pallas_call | solution.py:390
  46.2 0.0 copy-start.1
  46.2 0.0 copy-start
  46.2 1.9 %copy.16 = bf16[256,1024]{1,0:T(8,128)(2,1)} copy(bf16[256,1024]{1,0:T(8,128)(2,1)} %get-tuple-element.8) | data formatting | bytes 1048576
  48.1 1.9 %copy.17 = bf16[256,1024]{1,0:T(8,128)(2,1)} copy(bf16[256,1024]{1,0:T(8,128)(2,1)} %get-tuple-element.9) | data formatting | bytes 1048576
  49.9 0.0 copy-done.1
  50.0 0.6 %copy.18 = bf16[256,128]{1,0:T(8,128)(2,1)} copy(bf16[256,128]{1,0:T(8,128)(2,1)S(1)} %copy-done.1) | data formatting | bytes 131072
  50.6 0.0 copy-done
  50.6 0.6 %copy.19 = bf16[256,128]{1,0:T(8,128)(2,1)} copy(bf16[256,128]{1,0:T(8,128)(2,1)S(1)} %copy-done) | data formatting | bytes 131072
Async XLA Ops:
  46.2 3.8 %copy-start.1 = (bf16[256,128]{1,0:T(8,128)(2,1)S(1)}, bf16[256,128]{1,0:T(8,128)(2,1)}, u32[]{:S(2)}) copy-start(bf16[256,128]{1,0:T(8,128)(2,1)} %get-tuple-element.10) | copy-start | bytes 196612
  46.2 4.4 %copy-start = (bf16[256,128]{1,0:T(8,128)(2,1)S(1)}, bf16[256,128]{1,0:T(8,128)(2,1)}, u32[]{:S(2)}) copy-start(bf16[256,128]{1,0:T(8,128)(2,1)} %get-tuple-element.11) | copy-start | bytes 196612

commit v2 on v1

--- a/solution.py
+++ b/solution.py
@@ -57,18 +57,22 @@
     group = q_v.shape[1] // HD
     width = own_part.shape[2]
     rows = MEM // CHUNKS
-    half_t, half_s = tensors // 2, seqs // 2
+    half_t, groups = tensors // 2, seqs // 4
     si, ti = lax.axis_index("seq"), lax.axis_index("tensor")
-    zi, yi = si // 2, si % 2
+    gi, ri, yi = si // 4, (si // 2) % 2, si % 2
     xi, ci = ti // 2, ti % 2
-    y = yi.astype(F32)
-    n_y = 1.0 - y
+    y, r = yi.astype(F32), ri.astype(F32)
+    n_y, n_r = 1.0 - y, 1.0 - r
     core_dev = {"seq": si, "tensor": xi * 2 + (1 - ci)}
-    y_dev = {"seq": zi * 2 + (1 - yi), "tensor": ti}
-    up_dev = {"seq": (si + 2) % seqs, "tensor": ti}
-    down_dev = {"seq": (si + seqs - 2) % seqs, "tensor": ti}
+    y_dev = {"seq": gi * 4 + ri * 2 + (1 - yi), "tensor": ti}
+    row_devs = [{"seq": gi * 4 + (1 - ri) * 2 + where, "tensor": ti} for where in (yi, 1 - yi)]
+    group_devs = [y_dev] + row_devs
+    after, before = (gi + 1) % groups, (gi + groups - 1) % groups
+    up_devs = [{"seq": after * 4 + row * 2 + yi, "tensor": ti} for row in (1, 0)]
+    down_devs = [{"seq": before * 4 + row * 2 + yi, "tensor": ti} for row in (0, 1)]
     x_devs = [{"seq": si, "tensor": ((xi + 1 + n) % half_t) * 2 + ci} for n in range(half_t - 1)]
-    has_down, has_up = zi > 0, zi < half_s - 1
+    has_down, has_up = gi > 0, gi < groups - 1
+    sends_up, sends_down = has_up & (ri == 1), has_down & (ri == 0)
 
     def remote(src, dst, send, recv, device):
         return pltpu.make_async_remote_copy(
@@ -93,17 +97,16 @@
         pl.semaphore_signal(barrier, inc=1, device_id=device, device_id_type=pl.DeviceIdType.MESH)
 
     greet(core_dev)
-    greet(y_dev)
-    for device in x_devs:
+    for device in group_devs + x_devs:
         greet(device)
 
     @pl.when(has_down)
     def _():
-        greet(down_dev)
+        greet(down_devs[1])
 
     @pl.when(has_up)
     def _():
-        greet(up_dev)
+        greet(up_devs[1])
 
     dec_own[...] = jnp.broadcast_to(decay_ref[...], dec_own.shape)
 
@@ -142,10 +145,12 @@
     def proj_rows(block):
         return mp_v[pl.ds(pl.multiple_of(block * width, width), width), :]
 
-    chained = jnp.minimum(zi, 1) + jnp.minimum(half_s - 1 - zi, 1)
-    pl.semaphore_wait(barrier, 2 + len(x_devs) + chained)
+    chained = 2 * (ri * jnp.minimum(groups - 1 - gi, 1) + (1 - ri) * jnp.minimum(gi, 1))
+    pl.semaphore_wait(barrier, 1 + len(group_devs) + len(x_devs) + chained)
 
     sent = []
+    row_sent = []
+    row_back = []
     up_sent = []
     down_sent = []
 
@@ -154,7 +159,14 @@
         copy.start()
         sent.append(copy)
 
-    send(dec_own, dec_peer, dec_s.at[0], dec_r.at[0], y_dev)
+    def row_pair(own, peers, send_sems, recv_sems, c):
+        return [
+            remote(own.at[c], peers.at[1 + n, c], send_sems.at[1 + n, c], recv_sems.at[1 + n, c], row_devs[n])
+            for n in range(2)
+        ]
+
+    for n, device in enumerate(group_devs):
+        send(dec_own, dec_peer.at[n], dec_s.at[n], dec_r.at[n], device)
 
     for n in range(half_t):
         there = (xi + 1 + n) % half_t
@@ -195,38 +207,60 @@
             remote(x_send.at[n, c], x_recv.at[n, c], x_s.at[n, c], x_r.at[n, c], x_devs[n]).wait_recv()
             total = total + x_recv[n, c]
         w_own[c] = total
-        send(w_own.at[c], w_peer.at[c], y_s.at[c], y_r.at[c], y_dev)
+        send(w_own.at[c], w_peer.at[0, c], y_s.at[0, c], y_r.at[0, c], y_dev)
+        row_copies = row_pair(w_own, w_peer, y_s, y_r, c)
+
+        @pl.when(ri == 0)
+        def _():
+            for copy in row_copies:
+                copy.start()
+
+        row_sent.extend(row_copies)
 
     heads_loop(group // 2, group, 2, own_head)
 
-    remote(dec_own, dec_peer, dec_s.at[0], dec_r.at[0], y_dev).wait_recv()
-    mine = dec_own[0:1, :]
-    peer = dec_peer[0:1, :]
-    both = mine * peer
-
-    @pl.when(zi == 0)
+    for n, device in enumerate(group_devs):
+        remote(dec_own, dec_peer.at[n], dec_s.at[n], dec_r.at[n], device).wait_recv()
+    mine, peer, same, cross = dec_own[0:1, :], dec_peer[0, 0:1, :], dec_peer[1, 0:1, :], dec_peer[2, 0:1, :]
+    both, other = mine * peer, same * cross
+
+    @pl.when(gi == 0)
     def _():
         e_recv[...] = jnp.zeros_like(e_recv)
+
+    @pl.when(ri == 0)
+    def _():
+        w_peer[1] = jnp.zeros(w_peer.shape[1:], F32)
+        w_peer[2] = jnp.zeros(w_peer.shape[1:], F32)
 
     for c in range(CHUNKS):
         at = slice(c * rows, (c + 1) * rows)
-        remote(w_own.at[c], w_peer.at[c], y_s.at[c], y_r.at[c], y_dev).wait_recv()
-        from_peer = w_peer[c]
+        remote(w_own.at[c], w_peer.at[0, c], y_s.at[0, c], y_r.at[0, c], y_dev).wait_recv()
+        row_copies = row_pair(w_own, w_peer, y_s, y_r, c)
+
+        @pl.when(ri == 1)
+        def _():
+            for copy in row_copies:
+                copy.wait_recv()
+
+        from_peer = w_peer[0, c]
         pair = (n_y * peer + y) * w_own[c] + (n_y + y * mine) * from_peer
-        chain = remote(e_send.at[c], e_recv.at[c], z_s.at[c], z_r.at[c], up_dev)
+        earlier = (n_y * cross + y) * w_peer[1, c] + (n_y + y * same) * w_peer[2, c]
+        chain = [remote(e_send.at[c], e_recv.at[c], z_s.at[n, c], z_r.at[c], up_devs[n]) for n in range(2)]
 
         @pl.when(has_down)
         def _():
-            chain.wait_recv()
-
-        entering = e_recv[c]
+            chain[0].wait_recv()
+
+        entering = (n_r + r * other) * e_recv[c] + r * earlier
         e_send[c] = both * entering + pair
 
-        @pl.when(has_up)
-        def _():
-            chain.start()
-
-        up_sent.append(chain)
+        @pl.when(sends_up)
+        def _():
+            for copy in chain:
+                copy.start()
+
+        up_sent.extend(chain)
         state = (n_y + y * peer) * entering + y * from_peer
         state_v[at, :] = state
         for part, out in ((0, mk_v), (1, mv_v)):
@@ -271,7 +305,15 @@
         at = slice(c * rows, (c + 1) * rows)
         for part in range(2):
             ds_own[c, :, part * HD : (part + 1) * HD] = d_state[part][at, :]
-        send(ds_own.at[c], ds_peer.at[c], by_s.at[c], by_r.at[c], y_dev)
+        send(ds_own.at[c], ds_peer.at[0, c], by_s.at[0, c], by_r.at[0, c], y_dev)
+        row_copies = row_pair(ds_own, ds_peer, by_s, by_r, c)
+
+        @pl.when(ri == 1)
+        def _():
+            for copy in row_copies:
+                copy.start()
+
+        row_back.extend(row_copies)
 
     dk_v[...] = jnp.zeros_like(dk_v)
     dv_v[...] = jnp.zeros_like(dv_v)
@@ -288,28 +330,42 @@
 
     heads_loop(0, group // 2, 2, grad_head)
 
-    @pl.when(zi == half_s - 1)
+    @pl.when(gi == groups - 1)
     def _():
         b_recv[...] = jnp.zeros_like(b_recv)
 
+    @pl.when(ri == 1)
+    def _():
+        ds_peer[1] = jnp.zeros(ds_peer.shape[1:], F32)
+        ds_peer[2] = jnp.zeros(ds_peer.shape[1:], F32)
+
     for c in range(CHUNKS):
-        remote(ds_own.at[c], ds_peer.at[c], by_s.at[c], by_r.at[c], y_dev).wait_recv()
-        from_peer = ds_peer[c]
+        remote(ds_own.at[c], ds_peer.at[0, c], by_s.at[0, c], by_r.at[0, c], y_dev).wait_recv()
+        row_copies = row_pair(ds_own, ds_peer, by_s, by_r, c)
+
+        @pl.when(ri == 0)
+        def _():
+            for copy in row_copies:
+                copy.wait_recv()
+
+        from_peer = ds_peer[0, c]
         pair = (y * peer + n_y) * ds_own[c] + (n_y * mine + y) * from_peer
-        chain = remote(b_send.at[c], b_recv.at[c], bz_s.at[c], bz_r.at[c], down_dev)
+        later = (y * cross + n_y) * ds_peer[1, c] + (n_y * same + y) * ds_peer[2, c]
+        chain = [remote(b_send.at[c], b_recv.at[c], bz_s.at[n, c], bz_r.at[c], down_devs[n]) for n in range(2)]
 
         @pl.when(has_up)
         def _():
-            chain.wait_recv()
-
-        entering = b_recv[c]
+            chain[0].wait_recv()
+
+        entering = (r + n_r * other) * b_recv[c] + n_r * later
         b_send[c] = pair + both * entering
 
-        @pl.when(has_down)
-        def _():
-            chain.start()
-
-        down_sent.append(chain)
+        @pl.when(sends_down)
+        def _():
+            for copy in chain:
+                copy.start()
+
+        down_sent.extend(chain)
         at = slice(c * rows, (c + 1) * rows)
         r_own[at, :] = (y + n_y * peer) * entering + n_y * from_peer
         for n in range(half_t - 1):
@@ -360,14 +416,14 @@
 
     for copy in sent:
         copy.wait_send()
-    for copy in up_sent:
-        @pl.when(has_up)
-        def _():
-            copy.wait_send()
-    for copy in down_sent:
-        @pl.when(has_down)
-        def _():
-            copy.wait_send()
+    for ends, copies in (
+        (sends_up, up_sent), (sends_down, down_sent), (ri == 0, row_sent), (ri == 1, row_back)
+    ):
+        @pl.when(ends)
+        def _():
+            for copy in copies:
+                copy.wait_send()
+
     for store in stores:
         store.wait()
 
@@ -379,7 +435,7 @@
     half_t = tensors // 2
     rows = MEM // CHUNKS
     assert keys.shape[1] == HD and width == 2 * HD
-    assert seqs % 2 == 0 and tensors % 2 == 0
+    assert seqs % 4 == 0 and tensors % 2 == 0
     vmem = pl.BlockSpec(memory_space=pltpu.VMEM)
     anywhere = pl.BlockSpec(memory_space=pl.ANY)
     like = lambda a: pltpu.VMEM(a.shape, a.dtype)
@@ -387,6 +443,7 @@
     b16 = lambda *shape: pltpu.VMEM(shape, BF16)
     dma = lambda *shape: pltpu.SemaphoreType.DMA(shape)
     chunk = f32(CHUNKS, rows, width)
+    chunks3 = f32(3, CHUNKS, rows, width)
     return pl.pallas_call(
         functools.partial(kernel, seqs, tensors),
         out_shape=tuple(jax.ShapeDtypeStruct(a.shape, BF16) for a in (grad_out, queries, keys, values)),
@@ -404,16 +461,16 @@
             b16(group, MEM, seg), b16(group, MEM, seg), f32(group, 1, seg), f32(group, 1, seg),
             f32(half_t, MEM, width), f32(half_t, MEM, width), f32(half_t, MEM, width),
             f32(max(half_t - 1, 1), CHUNKS, rows, width), f32(max(half_t - 1, 1), CHUNKS, rows, width),
-            f32(8, width), f32(8, width), chunk, chunk, chunk, chunk,
+            f32(8, width), f32(3, 8, width), chunk, chunks3, chunk, chunk,
             f32(MEM, width), b16(MEM, HD), b16(MEM, HD), f32(MEM, HD), f32(MEM, HD),
-            chunk, chunk, chunk, chunk,
+            chunk, chunks3, chunk, chunk,
             f32(MEM, width), f32(max(half_t - 1, 1), MEM, width), f32(half_t, MEM, width),
             like(mem_queries), f32(seg, HD), f32(seg, HD),
             dma(6), dma(2),
             dma(half_t), dma(half_t),
             dma(max(half_t - 1, 1), CHUNKS), dma(max(half_t - 1, 1), CHUNKS),
-            dma(1), dma(1), dma(CHUNKS), dma(CHUNKS), dma(CHUNKS), dma(CHUNKS),
-            dma(CHUNKS), dma(CHUNKS), dma(CHUNKS), dma(CHUNKS),
+            dma(3), dma(3), dma(3, CHUNKS), dma(3, CHUNKS), dma(2, CHUNKS), dma(CHUNKS),
+            dma(3, CHUNKS), dma(3, CHUNKS), dma(2, CHUNKS), dma(CHUNKS),
             dma(max(half_t - 1, 1), CHUNKS), dma(max(half_t - 1, 1), CHUNKS),
             dma(half_t, CHUNKS), dma(half_t, CHUNKS),
         ],

time: 51.4 us -> 46.4 us (0.903)
  Pallas kernels: 45.5 us -> 40.5 us
    pallas_call x1, Pallas kernels: 45.5 us -> 40.5 us  [local(): pl.pallas_call(functools.partial(kernel, seqs, tensors), out_shape=tuple(...]
where the time goes in v2:
time: 46.4 us; the launch traced here: 46.2 us
  Pallas kernels  40.5 us (87%)
  local copies, waits for them, and re-layouts  5.04 us (11%)
  between operations  0.66 us (1%)
    pallas_call x1, Pallas kernels, local(): pl.pallas_call(functools.partial(kernel, seqs, tensors), out_shape=tuple(...  40.5 us
    unnamed x8, local copies, waits for them, and re-layouts  5.04 us

profile of v2, /device:TPU:1, one launch (start us, length us, event | category | flops | bytes accessed | tf_op | source)
XLA Modules:
  0.0 46.2 jit_solution(17493009196227711248)
XLA Ops:
  0.6 40.5 %shard_map.111 = (bf16[256,1024]{1,0:T(8,128)(2,1)}, bf16[256,1024]{1,0:T(8,128)(2,1)}, bf16[256,128]{1,0:T(8,128)(2,1)}, bf16[256,128]{1,0:T(8,128)(2,1)}) custom-call(bf16[256,1024]{1,0:T(8,128)(2,1)} %q_hbm.1, bf16[256,128]{1,0:T(8,128)(2,1)} %k_hbm.1, bf16[256,128]{1,0:T(8,128)(2,1)} %v_hbm.1, bf16[128,1024]{1,0:T(8,128)(2,1)} %mq_hbm.1, ...), custom_call_target="tpu_custom_call" | custom-call | tf_op jit(solution)/shard_map/pallas_call | solution.py:447
  41.1 0.0 copy-start.1
  41.1 0.0 copy-start
  41.1 1.9 %copy.16 = bf16[256,1024]{1,0:T(8,128)(2,1)} copy(bf16[256,1024]{1,0:T(8,128)(2,1)} %get-tuple-element.8) | data formatting | bytes 1048576
  43.0 1.9 %copy.17 = bf16[256,1024]{1,0:T(8,128)(2,1)} copy(bf16[256,1024]{1,0:T(8,128)(2,1)} %get-tuple-element.9) | data formatting | bytes 1048576
  44.9 0.0 copy-done.1
  44.9 0.6 %copy.18 = bf16[256,128]{1,0:T(8,128)(2,1)} copy(bf16[256,128]{1,0:T(8,128)(2,1)S(1)} %copy-done.1) | data formatting | bytes 131072
  45.5 0.0 copy-done
  45.5 0.6 %copy.19 = bf16[256,128]{1,0:T(8,128)(2,1)} copy(bf16[256,128]{1,0:T(8,128)(2,1)S(1)} %copy-done) | data formatting | bytes 131072
Async XLA Ops:
  41.1 3.8 %copy-start.1 = (bf16[256,128]{1,0:T(8,128)(2,1)S(1)}, bf16[256,128]{1,0:T(8,128)(2,1)}, u32[]{:S(2)}) copy-start(bf16[256,128]{1,0:T(8,128)(2,1)} %get-tuple-element.10) | copy-start | bytes 196612
  41.1 4.4 %copy-start = (bf16[256,128]{1,0:T(8,128)(2,1)S(1)}, bf16[256,128]{1,0:T(8,128)(2,1)}, u32[]{:S(2)}) copy-start(bf16[256,128]{1,0:T(8,128)(2,1)} %get-tuple-element.11) | copy-start | bytes 196612

commit v3 on v2

--- a/solution.py
+++ b/solution.py
@@ -428,6 +428,24 @@
         store.wait()
 
 
+def store_out(*refs):
+    sources, targets, held, (load_sem, store_sem) = refs[:4], refs[4:8], refs[8:12], refs[12:]
+    loads, stores = [], []
+    for n in range(4):
+        part = sources[n].shape[0] // 2
+        for i in range(2):
+            at = pl.ds(i * part, part)
+            loads.append(pltpu.make_async_copy(sources[n].at[at], held[n].at[at], load_sem.at[n, i]))
+            stores.append(pltpu.make_async_copy(held[n].at[at], targets[n].at[at], store_sem.at[n, i]))
+    for load in loads:
+        load.start()
+    for load, store in zip(loads, stores):
+        load.wait()
+        store.start()
+    for store in stores:
+        store.wait()
+
+
 def local(seqs, tensors, queries, keys, values, mem_queries, mem_proj, mem_decay, pattern, grad_out):
     seg, cols = queries.shape
     width = mem_decay.shape[1]
@@ -444,9 +462,10 @@
     dma = lambda *shape: pltpu.SemaphoreType.DMA(shape)
     chunk = f32(CHUNKS, rows, width)
     chunks3 = f32(3, CHUNKS, rows, width)
-    return pl.pallas_call(
+    shapes = tuple(jax.ShapeDtypeStruct(a.shape, BF16) for a in (grad_out, queries, keys, values))
+    results = pl.pallas_call(
         functools.partial(kernel, seqs, tensors),
-        out_shape=tuple(jax.ShapeDtypeStruct(a.shape, BF16) for a in (grad_out, queries, keys, values)),
+        out_shape=shapes,
         in_specs=[
             anywhere, anywhere, anywhere, anywhere, anywhere, vmem,
             pl.BlockSpec(memory_space=pltpu.SMEM), anywhere,
@@ -476,6 +495,13 @@
         ],
         compiler_params=pltpu.CompilerParams(collective_id=0, has_side_effects=True),
     )(queries, keys, values, mem_queries, mem_proj, mem_decay, pattern, grad_out)
+    return pl.pallas_call(
+        store_out,
+        out_shape=shapes,
+        in_specs=[anywhere] * 4,
+        out_specs=(anywhere,) * 4,
+        scratch_shapes=[like(a) for a in shapes] + [dma(4, 2), dma(4, 2)],
+    )(*results)
 
 
 def solution(mesh):

time: 46.4 us -> 43.4 us (0.935)
  local copies, waits for them, and re-layouts: 5.04 us -> 0 us
  Pallas kernels: 40.5 us -> 42.6 us
    unnamed x8 -> x0, local copies, waits for them, and re-layouts: 5.04 us -> none
    pallas_call x1 -> x2, Pallas kernels: 40.5 us -> 42.6 us  [the longest x1 40.5 us: local(): pl.pallas_call(functools.partial(kernel, seqs, tensors), out_shape=shapes...]
where the time goes in v3:
time: 43.4 us; the launch traced here: 43.2 us
  Pallas kernels  42.6 us (98%)
  between operations  0.64 us (1%)
    pallas_call x1, Pallas kernels, local(): pl.pallas_call(functools.partial(kernel, seqs, tensors), out_shape=shapes...  40.5 us
    pallas_call x1, Pallas kernels, local(): pl.pallas_call(store_out, out_shape=shapes, in_specs=[anywhere] * 4, out_...  2.08 us

profile of v3, /device:TPU:1, one launch (start us, length us, event | category | flops | bytes accessed | tf_op | source)
XLA Modules:
  0.0 43.2 jit_solution(6176209673223186828)
XLA Ops:
  0.6 40.5 %shard_map.111 = (bf16[256,1024]{1,0:T(8,128)(2,1)}, bf16[256,1024]{1,0:T(8,128)(2,1)}, bf16[256,128]{1,0:T(8,128)(2,1)}, bf16[256,128]{1,0:T(8,128)(2,1)}) custom-call(bf16[256,1024]{1,0:T(8,128)(2,1)} %q_hbm.1, bf16[256,128]{1,0:T(8,128)(2,1)} %k_hbm.1, bf16[256,128]{1,0:T(8,128)(2,1)} %v_hbm.1, bf16[128,1024]{1,0:T(8,128)(2,1)} %mq_hbm.1, ...), custom_call_target="tpu_custom_call" | custom-call | tf_op jit(solution)/shard_map/pallas_call | solution.py:466
  41.1 2.1 %shard_map.112 = (bf16[256,1024]{1,0:T(8,128)(2,1)}, bf16[256,1024]{1,0:T(8,128)(2,1)}, bf16[256,128]{1,0:T(8,128)(2,1)}, bf16[256,128]{1,0:T(8,128)(2,1)}) custom-call(bf16[256,1024]{1,0:T(8,128)(2,1)} %get-tuple-element.8.refs_0_, bf16[256,1024]{1,0:T(8,128)(2,1)} %get-tuple-element.9.refs_1_, bf16[256,128]{1,0:T(8,128)(2,1)} %get-tuple-element.10.refs_2_, ...), custom_call_target="tpu_custom_call" | custom-call | tf_op jit(solution)/shard_map/pallas_call | solution.py:498
